TPU v7x, 32 devices: a whole 2x2x4 slice. The times are simulated.
32 devices in a mesh: dp: 2 (over x), expert: 16 (over z, y, core).
Axes of the slice: x: 2, y: 2, z: 4, core: 2. Of those that a mesh axis runs over, the one named last changes fastest.
Arguments:
- q_latent: bfloat16 [128, 16, 576], P(('expert', 'dp')), may hold values from -48 to 48
- latent_cache: bfloat16 [128, 512, 576], P(('expert', 'dp')), may hold values from -10 to 10
- lengths: int32 [128], P(('expert', 'dp')), may hold values from 2 to 512
- residual: bfloat16 [128, 2048], P(('expert', 'dp')), may hold values from -6 to 6
- adapter_ids: int32 [128], P(('expert', 'dp')), may hold values from 0 to 31
- value_out: bfloat16 [8192, 2048], P('expert'), may hold values from -0.0625 to 0.0625
- adapter_down: bfloat16 [8192, 512], P('expert'), may hold values from -0.0625 to 0.0625
- adapter_up_factors: bfloat16 [512, 2048], P('expert'), may hold values from -1.5 to 1.5
- norm_gain: bfloat16 [2048], replicated, may hold values from 0.099609375 to 1.8984375
- expert_ids: int32 [128, 6], P('expert'), may hold values from 0 to 15, all different within a row; in each aligned block of 8 rows (0 to 7, 8 to 15, ...) at most 6 rows name the same one
- gate_weights: float32 [128, 6], P('expert'), may hold values from 0.05 to 0.5
- w_gate: bfloat16 [16, 2048, 1024], P('expert', None, 'dp'), may hold values from -0.125 to 0.125
- w_up: bfloat16 [16, 2048, 1024], P('expert', None, 'dp'), may hold values from -0.125 to 0.125
- w_down: bfloat16 [16, 2048, 1024], P('expert', None, 'dp'), may hold values from -0.1875 to 0.1875
Outputs:
- layer_out: bfloat16 [128, 2048], P(('expert', 'dp'))
Inputs may be any that keep to these rules, and one draw needn't show every extreme that they name: `expert_ids`: each row names 6 different experts. Requests e * 8 to e * 8 + 7 form aligned blocks; in each block no expert is named by more than 6 rows, and in some block an expert is named by exactly 6 rows.
All inputs are finite; a program needn't handle non-finite values.
Results may differ from a plain program's by a relative error of at most 0.008.
Values may be sent and summed in bfloat16 or wider, within the bound.
A program may use at most 64 MiB of HBM per device.

v0:
```python
import jax
import jax.numpy as jnp
from jax import lax
from jax.sharding import PartitionSpec as P

LAT = 512
ADAPTER_RANK = 16
SOFTMAX_SCALE = 192.0 ** (-0.5)
ADAPTER_SCALE = 2.0
EPSILON = 1e-06


def attend_one(query, latent_rows, length):
    scores = (
        lax.dot_general(
            query, latent_rows, (((1,), (1,)), ((), ())), preferred_element_type=jnp.float32
        )
        * SOFTMAX_SCALE
    )
    valid_mask = jnp.arange(latent_rows.shape[0], dtype=jnp.int32) < length
    scores = jnp.where(valid_mask[None, :], scores, -1e30)
    row_max = jnp.max(scores, axis=1, keepdims=True)
    raised = jnp.exp(scores - row_max)
    weights_bf = (raised / jnp.sum(raised, axis=1, keepdims=True)).astype(jnp.bfloat16)
    return jnp.dot(weights_bf, latent_rows[:, :LAT], preferred_element_type=jnp.float32).astype(
        jnp.bfloat16
    )


def expert_rows(tokens, gate_part, up_part, down_part):
    gate_act = jnp.dot(tokens, gate_part, preferred_element_type=jnp.float32)
    up_act = jnp.dot(tokens, up_part, preferred_element_type=jnp.float32)
    hidden_bf = (jax.nn.silu(gate_act) * up_act).astype(jnp.bfloat16)
    return lax.dot_general(
        hidden_bf, down_part, (((1,), (1,)), ((), ())), preferred_element_type=jnp.float32
    )


def local(
    q_latent,
    latent_cache,
    lengths,
    residual,
    adapter_ids,
    value_out,
    adapter_down,
    adapter_up_factors,
    norm_gain,
    expert_ids,
    gate_weights,
    w_gate,
    w_up,
    w_down,
):
    requests = residual.shape[0]
    model_width = residual.shape[1]
    head_count = q_latent.shape[1]
    latent_out = jax.vmap(attend_one)(q_latent, latent_cache, lengths).reshape(
        requests, head_count * LAT
    )
    pieces = lax.all_to_all(latent_out, "expert", split_axis=1, concat_axis=0, tiled=True)
    group_ids = lax.all_gather(adapter_ids, "expert", axis=0, tiled=True)
    group_rows = pieces.shape[0]
    adapters = adapter_down.shape[1] // ADAPTER_RANK
    owned_count = adapter_up_factors.shape[0] // ADAPTER_RANK
    down_projected_rows = jnp.dot(pieces, adapter_down, preferred_element_type=jnp.float32).reshape(
        group_rows, adapters, ADAPTER_RANK
    )
    chosen_adapters = group_ids[:, None] == jnp.arange(adapters, dtype=jnp.int32)[None, :]
    adapter_output = jnp.sum(
        jnp.where(chosen_adapters[:, :, None], down_projected_rows, 0.0), axis=1
    )
    adapter_down_rows = lax.psum(adapter_output, "expert")
    adapter_scaled_output = (ADAPTER_SCALE * adapter_down_rows).astype(jnp.bfloat16)
    first_owned = lax.axis_index("expert") * owned_count
    holder_mask = (
        group_ids[:, None] == first_owned + jnp.arange(owned_count, dtype=jnp.int32)[None, :]
    )
    spread_rows = jnp.where(
        holder_mask[:, :, None], adapter_scaled_output[:, None, :], jnp.zeros((), jnp.bfloat16)
    ).reshape(group_rows, owned_count * ADAPTER_RANK)
    attention = lax.psum_scatter(
        jnp.dot(pieces, value_out, preferred_element_type=jnp.float32)
        + jnp.dot(spread_rows, adapter_up_factors, preferred_element_type=jnp.float32),
        "expert",
        scatter_dimension=0,
        tiled=True,
    )
    residual_flow = residual.astype(jnp.float32) + attention
    inverse_rms = lax.rsqrt(
        jnp.mean(residual_flow * residual_flow, axis=1, keepdims=True) + EPSILON
    )
    normed = (residual_flow * inverse_rms * norm_gain.astype(jnp.float32)).astype(jnp.bfloat16)
    column = lax.all_gather(normed, "dp", axis=0, tiled=True)
    tokens = column.shape[0]
    top_count = expert_ids.shape[1]
    experts = lax.axis_size("expert") * w_gate.shape[0]
    share_size = max(1, 2 * requests * top_count // experts)
    dp_count = lax.axis_size("dp")
    slot_count = share_size * dp_count
    member = expert_ids[:, :, None] == jnp.arange(experts, dtype=jnp.int32)[None, None, :]
    flat_hits = member.reshape(tokens * top_count, experts).astype(jnp.int32)
    slot_rank = jnp.sum((jnp.cumsum(flat_hits, axis=0) - 1) * flat_hits, axis=1).reshape(
        tokens, top_count
    )
    placed = member[:, :, :, None] & (
        slot_rank[:, :, None, None] == jnp.arange(slot_count, dtype=jnp.int32)[None, None, None, :]
    )
    routing = jnp.any(placed, axis=1).reshape(tokens, experts * slot_count)
    combine = jnp.sum(jnp.where(placed, gate_weights[:, :, None, None], 0.0), axis=1).reshape(
        tokens, experts * slot_count
    )
    routing_rows = routing.T.astype(jnp.bfloat16)
    outgoing = (
        jnp.dot(routing_rows, column, preferred_element_type=jnp.float32)
        .astype(jnp.bfloat16)
        .reshape(experts, slot_count, model_width)
    )
    arrived = lax.all_to_all(outgoing, "expert", split_axis=0, concat_axis=0, tiled=True)
    produced = expert_rows(arrived.reshape(-1, model_width), w_gate[0], w_up[0], w_down[0])
    partial_value = produced.reshape(arrived.shape[0], arrived.shape[1], model_width)
    returned = lax.all_to_all(
        partial_value.astype(jnp.bfloat16), "expert", split_axis=0, concat_axis=0, tiled=True
    ).astype(partial_value.dtype)
    routed_column = jnp.dot(
        combine,
        returned.reshape(experts * slot_count, model_width),
        precision=lax.Precision.HIGHEST,
        preferred_element_type=jnp.float32,
    )
    routed_sum = lax.psum_scatter(
        routed_column.astype(jnp.bfloat16), "dp", scatter_dimension=0, tiled=True
    ).astype(jnp.float32)
    return (residual_flow + routed_sum).astype(jnp.bfloat16)


def solution(mesh):
    in_specs = (
        P(("expert", "dp"), None, None),
        P(("expert", "dp"), None, None),
        P(("expert", "dp")),
        P(("expert", "dp"), None),
        P(("expert", "dp")),
        P("expert", None),
        P("expert", None),
        P("expert", None),
        P(),
        P("expert", None),
        P("expert", None),
        P("expert", None, "dp"),
        P("expert", None, "dp"),
        P("expert", None, "dp"),
    )
    out_specs = P(("expert", "dp"), None)
    return jax.shard_map(local, mesh=mesh, in_specs=in_specs, out_specs=out_specs, check_vma=False)
```

profile of v0, /device:TPU:0, one launch (start us, length us, event | category | flops | bytes accessed | tf_op | source)
XLA Modules:
  0.0 223.4 jit_solution(10527450560244738211)
XLA Ops:
  6.5 0.9 iota_compare_fusion.4
  7.4 2.1 fusion.17
  9.8 2.3 %fusion.19 = bf16[4,16,512]{2,1,0:T(8,128)(2,1)S(1)} fusion(bf16[4,512,576]{1,2,0:T(8,128)(2,1)} %param.15, f32[4,16]{1,0:T(4,128)S(1)} %fusion.31, f32[4,16,512]{2,1,0:T(8,128)S(1)} %fusion.17), kind=kOutput, calls=%fused_computation.21 | convolution fusion | flops 33686080 | bytes 2426880 | tf_op jit(solution)/shard_map/vmap()/dot_general | solution.py:25
  12.1 0.7 copy.29
  12.8 7.4 %all-to-all-start = ((bf16[4,16,512]{2,0,1:T(4,128)(2,1)}), bf16[4,16,512]{2,0,1:T(4,128)(2,1)S(1)}, u32[]{:S(2)}, u32[]{:S(2)}) async-start(bf16[4,16,512]{2,0,1:T(4,128)(2,1)} %copy.29), calls=%async_computation | async-start | bytes 131072 | tf_op jit(solution)/shard_map/all_to_all | solution.py:61
  20.4 0.6 fusion.30
  21.9 12.4 %all-reduce = s32[64]{0:T(128)S(1)} all-reduce(s32[64]{0:T(128)S(1)} %dynamic-update-slice), channel_id=1, replica_groups=mesh['dp'=2,'expert'=16] {'expert'}, use_global_device_ids=true, to_apply=%add | all-reduce | flops 64 | bytes 512
  35.7 30.0 %psum.7 = f32[64,16]{0,1:T(8,128)S(1)} all-reduce(f32[64,16]{0,1:T(8,128)S(1)} %fusion.16), channel_id=1, replica_groups=mesh['dp'=2,'expert'=16] {'expert'}, use_global_device_ids=true, to_apply=%region_3.4 | all-reduce | flops 1024 | bytes 8192 | tf_op jit(solution)/shard_map/psum | solution.py:73
  65.7 2.1 fusion.32
  67.8 1.1 convolution_add_fusion
  70.0 87.0 %all-reduce.5.cloned.1.call-done = f32[64,2048]{1,0:T(8,128)} async-done(((f32[64,2048]{1,0:T(8,128)}), f32[64,2048]{1,0:T(8,128)}) %all-reduce.5.cloned.1.call-update) | async-done | bytes 524304
  157.0 1.0 multiply_reduce_fusion
  158.0 0.9 fusion.28
  158.9 4.4 %all-gather = bf16[2,4,2048]{2,1,0:T(4,128)(2,1)S(1)} all-gather(bf16[1,4,2048]{2,1,0:T(4,128)(2,1)S(1)} %fusion.28), channel_id=1, replica_groups=mesh['dp'=2,'expert'=16] {'dp'}, dimensions={0}, use_global_device_ids=true | all-gather | bytes 49152 | tf_op jit(solution)/shard_map/all_gather | solution.py:94
  163.8 19.2 %all_to_all.26 = bf16[16,6,2048]{2,1,0:T(8,128)(2,1)S(1)} all-to-all(bf16[16,6,2048]{2,1,0:T(8,128)(2,1)S(1)} %reshape.122), channel_id=1, replica_groups=mesh['dp'=2,'expert'=16] {'expert'}, dimensions={0} | all-to-all | bytes 786432 | tf_op jit(solution)/shard_map/all_to_all | solution.py:119
  183.2 2.2 fusion.5
  186.0 0.8 convolution_convert_fusion
  186.7 1.0 copy.37
  187.8 4.2 %all-to-all-start.2 = ((bf16[16,6,2048]{2,1,0:T(8,128)(2,1)}), bf16[16,6,2048]{2,1,0:T(8,128)(2,1)S(1)}, u32[]{:S(2)}, u32[]{:S(2)}) async-start(bf16[16,6,2048]{2,1,0:T(8,128)(2,1)} %copy.37), calls=%async_computation.2 | async-start | bytes 1048576 | tf_op jit(solution)/shard_map/all_to_all | solution.py:122
  192.0 0.6 dynamic-slice.3
  193.4 12.8 %all-to-all-done.2 = bf16[16,6,2048]{2,1,0:T(8,128)(2,1)S(1)} async-done(((bf16[16,6,2048]{2,1,0:T(8,128)(2,1)}), bf16[16,6,2048]{2,1,0:T(8,128)(2,1)S(1)}, u32[]{:S(2)}, u32[]{:S(2)}) %all-to-all-start.2) | async-done | bytes 393248 | tf_op jit(solution)/shard_map/all_to_all | solution.py:122
  206.2 0.6 fusion.1
  206.8 8.3 %all-reduce.2 = bf16[8,2048]{1,0:T(8,128)(2,1)S(1)} all-reduce(bf16[8,2048]{1,0:T(8,128)(2,1)S(1)} %fusion.1), channel_id=3, replica_groups=mesh['dp'=2,'expert'=16] {'dp'}, use_global_device_ids=true, to_apply=%region_10.11.clone | all-reduce | flops 16384 | bytes 65536
  215.1 1.5 add_convert_fusion
  (59 shorter events, 3.8 us)
Async XLA Ops:
  6.5 179.4 %copy-start = (bf16[1,2048,512]{2,1,0:T(8,128)(2,1)S(1)}, bf16[1,2048,512]{2,1,0:T(8,128)(2,1)}, u32[]{:S(2)}) copy-start(bf16[1,2048,512]{2,1,0:T(8,128)(2,1)} %param.27) | copy-start | bytes 6291460
  9.6 10.7 %copy-start.4 = (s32[8,6]{1,0:T(8,128)S(1)}, s32[8,6]{1,0:T(8,128)}, u32[]{:S(2)}) copy-start(s32[8,6]{1,0:T(8,128)} %param.23) | copy-start | bytes 580
  9.6 10.8 %copy-start.7 = (u32[32]{0:T(128)S(1)}, u32[32]{0:T(128)}, u32[]{:S(2)}) copy-start(u32[32]{0:T(128)} %constant.49) | copy-start | bytes 388
  9.6 12.1 %copy-start.9 = (s32[4]{0:T(128)S(1)}, s32[4]{0:T(128)}, u32[]{:S(2)}) copy-start(s32[4]{0:T(128)} %param.18) | copy-start | bytes 52
  9.6 24.7 %copy-start.1 = (bf16[512,512]{1,0:T(8,128)(2,1)S(1)}, bf16[512,512]{1,0:T(8,128)(2,1)}, u32[]{:S(2)}) copy-start(bf16[512,512]{1,0:T(8,128)(2,1)} %param.20) | copy-start | bytes 1572868
  9.6 25.0 %copy-start.5 = (bf16[2048]{0:T(1024)(128)(2,1)S(1)}, bf16[2048]{0:T(1024)(128)(2,1)}, u32[]{:S(2)}) copy-start(bf16[2048]{0:T(1024)(128)(2,1)} %param.22) | copy-start | bytes 12292
  12.8 22.4 %all-to-all-start = ((bf16[4,16,512]{2,0,1:T(4,128)(2,1)}), bf16[4,16,512]{2,0,1:T(4,128)(2,1)S(1)}, u32[]{:S(2)}, u32[]{:S(2)}) async-start(bf16[4,16,512]{2,0,1:T(4,128)(2,1)} %copy.29), calls=%async_computation | async-start | bytes 131072 | tf_op jit(solution)/shard_map/all_to_all | solution.py:61
  20.2 136.8 %all-reduce.5.cloned.1.call-start = ((), (), s32[]{:S(2)}) async-start(), calls=%async_computation.3 | async-start | bytes 1048576
  34.5 33.3 %copy-start.3 = (bf16[32,2048]{1,0:T(8,128)(2,1)S(1)}, bf16[32,2048]{1,0:T(8,128)(2,1)}, u32[]{:S(2)}) copy-start(bf16[32,2048]{1,0:T(8,128)(2,1)} %param.21) | copy-start | bytes 393220
  65.7 91.3 %copy-start.2 = (bf16[4,2048]{1,0:T(4,128)(2,1)S(1)}, bf16[4,2048]{1,0:T(4,128)(2,1)}, u32[]{:S(2)}) copy-start(bf16[4,2048]{1,0:T(4,128)(2,1)} %param.17) | copy-start | bytes 49156
  183.2 2.2 copy-start.8
  185.9 6.0 %copy-start.6 = (f32[8,6]{1,0:T(8,128)S(1)}, f32[8,6]{1,0:T(8,128)}, u32[]{:S(2)}) copy-start(f32[8,6]{1,0:T(8,128)} %param.24) | copy-start | bytes 580
  185.9 6.1 %copy-start.10 = (u32[32]{0:T(128)S(1)}, u32[32]{0:T(128)}, u32[]{:S(2)}) copy-start(u32[32]{0:T(128)} %constant.59) | copy-start | bytes 388
  187.8 18.4 %all-to-all-start.2 = ((bf16[16,6,2048]{2,1,0:T(8,128)(2,1)}), bf16[16,6,2048]{2,1,0:T(8,128)(2,1)S(1)}, u32[]{:S(2)}, u32[]{:S(2)}) async-start(bf16[16,6,2048]{2,1,0:T(8,128)(2,1)} %copy.37), calls=%async_computation.2 | async-start | bytes 1048576 | tf_op jit(solution)/shard_map/all_to_all | solution.py:122
Sparse Core Ops, SparseCore 0:
  69.0 87.9 all-reduce.4
where the time goes:
time: 224 us; the launch traced here: 223 us
  waiting for transfers between devices  99.8 us (45%)
  blocking collectives  74.4 us (33%)
  between operations  15.6 us (7%)
  matrix products  12.3 us (5%)
  starting transfers between devices  11.6 us (5%)
  other arithmetic  5.19 us (2%)
  local copies, waits for them, and re-layouts  4.47 us (2%)
    unnamed x2, waiting for transfers between devices  87 us
    psum x1, blocking collectives, local(): adapter_down_rows = lax.psum(adapter_output, 'expert')  30 us
    unnamed x2, blocking collectives  20.7 us
    all_to_all x1, blocking collectives, local(): lax.all_to_all(outgoing, 'expert', split_axis=0, concat_axis=0, tiled=True)  19.2 us
    all_to_all x1, waiting for transfers between devices, local(): lax.all_to_all(partial_value.astype(jnp.bfloat16), 'expert', split_axis=0...  12.8 us
    all_to_all x1, starting transfers between devices, local(): lax.all_to_all(latent_out, 'expert', split_axis=1, concat_axis=0, tiled=T...  7.41 us
  transfers between devices with their start and end apart: 3, of which 2 were waited for; matrix products, arithmetic and copies ran while one was open for 1% of the time, Pallas kernels for 0%

commit v1 on v0

--- a/solution.py
+++ b/solution.py
@@ -8,6 +8,15 @@
 SOFTMAX_SCALE = 192.0 ** (-0.5)
 ADAPTER_SCALE = 2.0
 EPSILON = 1e-06
+
+
+def manage_words(unit, a_name):
+    n_axis = lax.axis_size(a_name)
+    mid_arr = lambda right_arr: [(d, d ^ right_arr) for d in range(n_axis)]
+    view_out = unit
+    for pp in range(n_axis.bit_length() - 1):
+        view_out = view_out + lax.ppermute(view_out, a_name, mid_arr(1 << pp))
+    return view_out
 
 
 def attend_one(query, latent_rows, length):
@@ -70,7 +79,7 @@
     adapter_output = jnp.sum(
         jnp.where(chosen_adapters[:, :, None], down_projected_rows, 0.0), axis=1
     )
-    adapter_down_rows = lax.psum(adapter_output, "expert")
+    adapter_down_rows = manage_words(adapter_output, "expert")
     adapter_scaled_output = (ADAPTER_SCALE * adapter_down_rows).astype(jnp.bfloat16)
     first_owned = lax.axis_index("expert") * owned_count
     holder_mask = (

time: 224 us -> 205 us (0.915)
  blocking collectives: 74.4 us -> 44.4 us
  waiting for transfers between devices: 99.8 us -> 109 us
    psum x1 -> x0, blocking collectives: 30 us -> none  [local(): adapter_down_rows = lax.psum(adapter_output, 'expert')]
    ppermute x0 -> x4, waiting for transfers between devices: none -> 8.87 us  [manage_words(): view_out = view_out + lax.ppermute(view_out, a_name, mid_arr(1 << pp))]
  transfers between devices with their start and end apart: 3 -> 7, of which waited for: 2 -> 6; matrix products, arithmetic and copies ran while one was open for 1% -> 2% of each run, Pallas kernels for 0% -> 0%
where the time goes in v1:
time: 205 us
  waiting for transfers between devices  109 us (53%)
  blocking collectives  44.4 us (22%)
  between operations  15.6 us (8%)
  starting transfers between devices  13.6 us (7%)
  matrix products  12.3 us (6%)
  other arithmetic  5.19 us (3%)
  local copies, waits for them, and re-layouts  4.47 us (2%)
    unnamed x2, waiting for transfers between devices  87.3 us
    unnamed x2, blocking collectives  20.7 us
    all_to_all x1, blocking collectives, local(): lax.all_to_all(outgoing, 'expert', split_axis=0, concat_axis=0, tiled=True)  19.2 us
    all_to_all x1, waiting for transfers between devices, local(): lax.all_to_all(partial_value.astype(jnp.bfloat16), 'expert', split_axis=0...  12.8 us
    ppermute x4, waiting for transfers between devices, manage_words(): view_out = view_out + lax.ppermute(view_out, a_name, mid_arr(1 << pp))  8.87 us
    all_to_all x1, starting transfers between devices, local(): lax.all_to_all(latent_out, 'expert', split_axis=1, concat_axis=0, tiled=T...  7.41 us
    all_gather x1, blocking collectives, local(): column = lax.all_gather(normed, 'dp', axis=0, tiled=True)  4.41 us
    all_to_all x1, starting transfers between devices, local(): lax.all_to_all(partial_value.astype(jnp.bfloat16), 'expert', split_axis=0...  4.16 us
  transfers between devices with their start and end apart: 7, of which 6 were waited for; matrix products, arithmetic and copies ran while one was open for 2% of the time, Pallas kernels for 0%

profile of v1, /device:TPU:0, one launch (start us, length us, event | category | flops | bytes accessed | tf_op | source)
XLA Modules:
  0.0 204.5 jit_solution(9691120842002466263)
XLA Ops:
  6.5 0.9 iota_compare_fusion.4
  7.4 2.1 %fusion.17 = f32[4,16,512]{2,1,0:T(8,128)S(1)} fusion(bf16[4,16,576]{2,1,0:T(8,128)(2,1)} %param.14, bf16[4,512,576]{1,2,0:T(8,128)(2,1)} %param.15, pred[4,512]{1,0:T(4,128)(4,1)S(1)} %iota_compare_fusion.4), kind=kOutput, calls=%fused_computation.19 | convolution fusion | flops 37814272 | bytes 2566144 | tf_op jit(solution)/shard_map/vmap()/dot_general | solution.py:24
  9.8 2.3 %fusion.19 = bf16[4,16,512]{2,1,0:T(8,128)(2,1)S(1)} fusion(bf16[4,512,576]{1,2,0:T(8,128)(2,1)} %param.15, f32[4,16]{1,0:T(4,128)S(1)} %fusion.31, f32[4,16,512]{2,1,0:T(8,128)S(1)} %fusion.17), kind=kOutput, calls=%fused_computation.21 | convolution fusion | flops 33686080 | bytes 2426880 | tf_op jit(solution)/shard_map/vmap()/dot_general | solution.py:34
  12.8 7.4 %all-to-all-start = ((bf16[4,16,512]{2,0,1:T(4,128)(2,1)}), bf16[4,16,512]{2,0,1:T(4,128)(2,1)S(1)}, u32[]{:S(2)}, u32[]{:S(2)}) async-start(bf16[4,16,512]{2,0,1:T(4,128)(2,1)} %copy.29), calls=%async_computation | async-start | bytes 131072 | tf_op jit(solution)/shard_map/all_to_all | solution.py:70
  21.8 12.4 %all-reduce = s32[64]{0:T(128)S(1)} all-reduce(s32[64]{0:T(128)S(1)} %dynamic-update-slice), channel_id=1, replica_groups=mesh['dp'=2,'expert'=16] {'expert'}, use_global_device_ids=true, to_apply=%add | all-reduce | flops 64 | bytes 512
  35.6 1.1 collective-permute-done
  36.7 0.9 collective-permute-start.1
  37.6 2.8 %collective-permute-done.1 = f32[64,16]{0,1:T(8,128)S(1)} collective-permute-done((f32[64,16]{0,1:T(8,128)S(1)}, f32[64,16]{0,1:T(8,128)S(1)}, u32[]{:S(2)}, u32[]{:S(2)}) %collective-permute-start.1) | collective-permute-done | bytes 4128 | tf_op jit(solution)/shard_map/ppermute | solution.py:18
  41.1 2.9 %collective-permute-done.2 = f32[64,16]{0,1:T(8,128)S(1)} collective-permute-done((f32[64,16]{0,1:T(8,128)S(1)}, f32[64,16]{0,1:T(8,128)S(1)}, u32[]{:S(2)}, u32[]{:S(2)}) %collective-permute-start.2) | collective-permute-done | bytes 4128 | tf_op jit(solution)/shard_map/ppermute | solution.py:18
  44.6 2.1 %fusion.32 = f32[64,2048]{1,0:T(8,128)S(1)} fusion(bf16[64,512]{1,0:T(8,128)(2,1)S(1)} %all_to_all.20, bf16[512,2048]{1,0:T(8,128)(2,1)} %param.19), kind=kOutput, calls=%fused_computation.50 | convolution fusion | flops 134217728 | bytes 2686976 | tf_op jit(solution)/shard_map/dot_general | solution.py:92
  46.6 2.0 collective-permute-done.3
  48.7 1.1 convolution_add_fusion
  50.8 87.3 %all-reduce.5.cloned.1.call-done = f32[64,2048]{1,0:T(8,128)} async-done(((f32[64,2048]{1,0:T(8,128)}), f32[64,2048]{1,0:T(8,128)}) %all-reduce.5.cloned.1.call-update) | async-done | bytes 524304
  138.1 1.0 multiply_reduce_fusion
  139.1 0.9 fusion.28
  140.1 4.4 %all-gather = bf16[2,4,2048]{2,1,0:T(4,128)(2,1)S(1)} all-gather(bf16[1,4,2048]{2,1,0:T(4,128)(2,1)S(1)} %fusion.28), channel_id=1, replica_groups=mesh['dp'=2,'expert'=16] {'dp'}, dimensions={0}, use_global_device_ids=true | all-gather | bytes 49152 | tf_op jit(solution)/shard_map/all_gather | solution.py:103
  144.9 19.2 %all_to_all.26 = bf16[16,6,2048]{2,1,0:T(8,128)(2,1)S(1)} all-to-all(bf16[16,6,2048]{2,1,0:T(8,128)(2,1)S(1)} %reshape.122), channel_id=1, replica_groups=mesh['dp'=2,'expert'=16] {'expert'}, dimensions={0} | all-to-all | bytes 786432 | tf_op jit(solution)/shard_map/all_to_all | solution.py:128
  164.3 2.2 %fusion.5 = f32[96,512]{1,0:T(8,128)S(1)} fusion(bf16[96,2048]{1,0:T(8,128)(2,1)S(1)} %reshape.123, bf16[1,2048,512]{2,1,0:T(8,128)(2,1)} %param.25), kind=kOutput, calls=%fused_computation.9 | convolution fusion | flops 201326592 | bytes 2686976 | tf_op jit(solution)/shard_map/dot_general | solution.py:40
  167.1 0.8 convolution_convert_fusion
  167.9 1.0 copy.37
  168.9 4.2 %all-to-all-start.2 = ((bf16[16,6,2048]{2,1,0:T(8,128)(2,1)}), bf16[16,6,2048]{2,1,0:T(8,128)(2,1)S(1)}, u32[]{:S(2)}, u32[]{:S(2)}) async-start(bf16[16,6,2048]{2,1,0:T(8,128)(2,1)} %copy.37), calls=%async_computation.2 | async-start | bytes 1048576 | tf_op jit(solution)/shard_map/all_to_all | solution.py:131
  174.5 12.8 %all-to-all-done.2 = bf16[16,6,2048]{2,1,0:T(8,128)(2,1)S(1)} async-done(((bf16[16,6,2048]{2,1,0:T(8,128)(2,1)}), bf16[16,6,2048]{2,1,0:T(8,128)(2,1)S(1)}, u32[]{:S(2)}, u32[]{:S(2)}) %all-to-all-start.2) | async-done | bytes 393248 | tf_op jit(solution)/shard_map/all_to_all | solution.py:131
  187.9 8.3 %all-reduce.2 = bf16[8,2048]{1,0:T(8,128)(2,1)S(1)} all-reduce(bf16[8,2048]{1,0:T(8,128)(2,1)S(1)} %fusion.1), channel_id=3, replica_groups=mesh['dp'=2,'expert'=16] {'dp'}, use_global_device_ids=true, to_apply=%region_9.10.clone | all-reduce | flops 16384 | bytes 65536
  196.2 1.5 add_convert_fusion
  (69 shorter events, 7.4 us)
Async XLA Ops:
  6.5 160.5 %copy-start = (bf16[1,2048,512]{2,1,0:T(8,128)(2,1)S(1)}, bf16[1,2048,512]{2,1,0:T(8,128)(2,1)}, u32[]{:S(2)}) copy-start(bf16[1,2048,512]{2,1,0:T(8,128)(2,1)} %param.27) | copy-start | bytes 6291460
  9.6 10.7 %copy-start.7 = (u32[32]{0:T(128)S(1)}, u32[32]{0:T(128)}, u32[]{:S(2)}) copy-start(u32[32]{0:T(128)} %constant.49) | copy-start | bytes 388
  9.6 11.9 %copy-start.9 = (s32[4]{0:T(128)S(1)}, s32[4]{0:T(128)}, u32[]{:S(2)}) copy-start(s32[4]{0:T(128)} %param.18) | copy-start | bytes 52
  9.6 24.6 %copy-start.1 = (bf16[512,512]{1,0:T(8,128)(2,1)S(1)}, bf16[512,512]{1,0:T(8,128)(2,1)}, u32[]{:S(2)}) copy-start(bf16[512,512]{1,0:T(8,128)(2,1)} %param.20) | copy-start | bytes 1572868
  9.6 24.8 %copy-start.4 = (s32[8,6]{1,0:T(8,128)S(1)}, s32[8,6]{1,0:T(8,128)}, u32[]{:S(2)}) copy-start(s32[8,6]{1,0:T(8,128)} %param.23) | copy-start | bytes 580
  9.8 31.3 %copy-start.5 = (bf16[2048]{0:T(1024)(128)(2,1)S(1)}, bf16[2048]{0:T(1024)(128)(2,1)}, u32[]{:S(2)}) copy-start(bf16[2048]{0:T(1024)(128)(2,1)} %param.22) | copy-start | bytes 12292
  12.8 22.2 %all-to-all-start = ((bf16[4,16,512]{2,0,1:T(4,128)(2,1)}), bf16[4,16,512]{2,0,1:T(4,128)(2,1)S(1)}, u32[]{:S(2)}, u32[]{:S(2)}) async-start(bf16[4,16,512]{2,0,1:T(4,128)(2,1)} %copy.29), calls=%async_computation | async-start | bytes 131072 | tf_op jit(solution)/shard_map/all_to_all | solution.py:70
  20.2 118.0 %all-reduce.5.cloned.1.call-start = ((), (), s32[]{:S(2)}) async-start(), calls=%async_computation.3 | async-start | bytes 1048576
  34.4 14.3 %copy-start.3 = (bf16[32,2048]{1,0:T(8,128)(2,1)S(1)}, bf16[32,2048]{1,0:T(8,128)(2,1)}, u32[]{:S(2)}) copy-start(bf16[32,2048]{1,0:T(8,128)(2,1)} %param.21) | copy-start | bytes 393220
  35.5 1.2 collective-permute-start
  36.7 3.7 %collective-permute-start.1 = (f32[64,16]{0,1:T(8,128)S(1)}, f32[64,16]{0,1:T(8,128)S(1)}, u32[]{:S(2)}, u32[]{:S(2)}) collective-permute-start(f32[64,16]{0,1:T(8,128)S(1)} %add.51), channel_id=1, source_target_pairs={{0,2},{1,3},{2,0},{3,1},{4,6},{5,7},{6,4},{7,5},{8,10},{9,11},{10,... | collective-permute-start | bytes 12296 | tf_op jit(solution)/shard_map/ppermute | solution.py:18
  40.4 3.7 %collective-permute-start.2 = (f32[64,16]{0,1:T(8,128)S(1)}, f32[64,16]{0,1:T(8,128)S(1)}, u32[]{:S(2)}, u32[]{:S(2)}) collective-permute-start(f32[64,16]{0,1:T(8,128)S(1)} %add.52), channel_id=1, source_target_pairs={{0,4},{1,5},{2,6},{3,7},{4,0},{5,1},{6,2},{7,3},{8,12},{9,13},{10,... | collective-permute-start | bytes 12296 | tf_op jit(solution)/shard_map/ppermute | solution.py:18
  44.0 94.1 %copy-start.2 = (bf16[4,2048]{1,0:T(4,128)(2,1)S(1)}, bf16[4,2048]{1,0:T(4,128)(2,1)}, u32[]{:S(2)}) copy-start(bf16[4,2048]{1,0:T(4,128)(2,1)} %param.17) | copy-start | bytes 49156
  44.0 4.6 %collective-permute-start.3 = (f32[64,16]{0,1:T(8,128)S(1)}, f32[64,16]{0,1:T(8,128)S(1)}, u32[]{:S(2)}, u32[]{:S(2)}) collective-permute-start(f32[64,16]{0,1:T(8,128)S(1)} %add.53), channel_id=1, source_target_pairs={{0,8},{1,9},{2,10},{3,11},{4,12},{5,13},{6,14},{7,15},{8,0},{9,1},... | collective-permute-start | bytes 12296 | tf_op jit(solution)/shard_map/ppermute | solution.py:18
  164.3 2.2 %copy-start.8 = (bf16[1,2048,512]{2,1,0:T(8,128)(2,1)S(1)}, bf16[1,2048,512]{2,1,0:T(8,128)(2,1)}, u32[]{:S(2)}) copy-start(bf16[1,2048,512]{2,1,0:T(8,128)(2,1)} %param.26) | copy-start | bytes 6291460
  167.1 6.0 %copy-start.6 = (f32[8,6]{1,0:T(8,128)S(1)}, f32[8,6]{1,0:T(8,128)}, u32[]{:S(2)}) copy-start(f32[8,6]{1,0:T(8,128)} %param.24) | copy-start | bytes 580
  167.1 6.1 %copy-start.10 = (u32[32]{0:T(128)S(1)}, u32[32]{0:T(128)}, u32[]{:S(2)}) copy-start(u32[32]{0:T(128)} %constant.59) | copy-start | bytes 388
  168.9 18.4 %all-to-all-start.2 = ((bf16[16,6,2048]{2,1,0:T(8,128)(2,1)}), bf16[16,6,2048]{2,1,0:T(8,128)(2,1)S(1)}, u32[]{:S(2)}, u32[]{:S(2)}) async-start(bf16[16,6,2048]{2,1,0:T(8,128)(2,1)} %copy.37), calls=%async_computation.2 | async-start | bytes 1048576 | tf_op jit(solution)/shard_map/all_to_all | solution.py:131
Sparse Core Ops, SparseCore 0:
  49.9 88.2 all-reduce.4
